TPU v7x, 256 devices: a whole 4x4x8 slice. The times are simulated.
256 devices in a mesh: tok: 32 (over z_hi, x, core), lyr: 8 (over z_lo, y).
Axes of the slice: x: 4, y: 4, z: 8 (z_hi: 4, z_lo: 2; z = z_hi * 2 + z_lo), core: 2. Of those that a mesh axis runs over, the one named last changes fastest.
Arguments:
- feature_codes: bfloat16 [16, 4096, 2, 256], P('lyr', 'tok'), may hold values from 0 to 21, as said below
- block_ids: int32 [16, 4096, 2], P('lyr', 'tok'), may hold values from 0 to 31, all different within a row; in each aligned block of 128 rows (0 to 127, 128 to 255, ..., all dimensions but the last counted through in order) at most 16 rows name the same one
- target_layer: int32 [4096], P('tok'), may hold values from 0 to 15
- request_ids: int32 [4096], P('tok'), may hold values from 0 to 15
- target_resid: bfloat16 [4096, 2304], P('tok'), may hold values from -6 to 6
- decoder: bfloat16 [16, 8192, 2304], P('lyr', 'tok'), may hold values from -0.25 to 0.25
Outputs:
- scores: bfloat16 [16, 4096, 2, 256], P('lyr', 'tok')
- request_totals: float32 [16, 16, 8192], P(None, 'lyr', 'tok')
Inputs may be any that keep to these rules, and one draw needn't show every extreme that they name: `block_ids`: the 2 panel indices of one token at one source layer are distinct; among the 128 tokens of one index of tok at one source layer no panel is named by more than 16 of them, a bound that some block reaches. `feature_codes`: nonnegative, with many entries zero.
All inputs are finite; a program needn't handle non-finite values.
Results may differ from a plain program's by a relative error of at most 0.0053.
Values may be sent and summed in bfloat16 or wider, within the bound.
No kernel may reach another device: no remote copies, remote signals or barrier semaphores. Data moves between devices by JAX's collectives and lax.ppermute only.
A program may use at most 64 MiB of HBM per device.

v0:
```python
import jax
import jax.numpy as jnp
from jax import lax
from jax.sharding import PartitionSpec as P

PANELS = 32
REQUESTS = 16
CAP = 16


def slot_of(flat_ids):
    one_hot = (flat_ids[:, None] == jnp.arange(PANELS, dtype=jnp.int32)[None, :]).astype(jnp.int32)
    before = jnp.cumsum(one_hot, axis=0) - one_hot
    return flat_ids * CAP + jnp.sum(before * one_hot, axis=1)


def source_of(slot_ids):
    row_count = slot_ids.shape[0]
    empty = jnp.full((PANELS * CAP,), row_count, jnp.int32)
    return empty.at[slot_ids].set(jnp.arange(row_count, dtype=jnp.int32))


def take_rows(table, index):
    return jnp.take(table, index, axis=0)


def pad_zero(table):
    return jnp.concatenate([table, jnp.zeros((1,) + table.shape[1:], table.dtype)], axis=0)


def normalize_error(resid_rows, rebuilt):
    error = resid_rows.astype(jnp.float32) - rebuilt
    spread = jnp.mean(error * error, axis=-1, keepdims=True)
    return (error * lax.rsqrt(spread + 1e-06)).astype(jnp.bfloat16)


def per_device(feature_codes, block_ids, target_layer, request_ids, target_resid, decoder):
    layers_here, count, kact, panel = feature_codes.shape
    width = target_resid.shape[1]
    tok_count = lax.axis_size("tok")
    per_dev = PANELS // tok_count
    rows_here = count * kact
    first_layer = lax.axis_index("lyr") * layers_here
    layer_ids = first_layer + jnp.arange(layers_here, dtype=jnp.int32)
    alive_mask = (layer_ids[:, None] <= target_layer[None, :]).astype(feature_codes.dtype)
    masked = feature_codes * alive_mask[:, :, None, None]
    flat_ids = block_ids.reshape(layers_here, rows_here)
    slot_ids = jax.vmap(slot_of)(flat_ids)
    source_rows = jax.vmap(source_of)(slot_ids)
    token_of = source_rows // kact
    code_rows = jax.vmap(pad_zero)(masked.reshape(layers_here, rows_here, panel))
    send_codes = jax.vmap(take_rows)(code_rows, source_rows).reshape(
        layers_here, tok_count, per_dev, CAP, panel
    )
    panel_weights = decoder.reshape(layers_here, per_dev, panel, width)
    received = lax.all_to_all(send_codes, "tok", split_axis=1, concat_axis=1, tiled=True)
    built = jnp.einsum(
        "lspcj,lpjd->lspcd", received, panel_weights, preferred_element_type=jnp.float32
    ).astype(jnp.bfloat16)
    returned = lax.all_to_all(built, "tok", split_axis=1, concat_axis=1, tiled=True).reshape(
        layers_here, PANELS * CAP, width
    )
    per_row = jax.vmap(take_rows)(returned, slot_ids)
    partial_value = jnp.sum(
        per_row.astype(jnp.float32).reshape(layers_here, count, kact, width), axis=(0, 2)
    )
    rebuilt = lax.psum(partial_value, "lyr")
    gradient = normalize_error(target_resid, rebuilt)
    send_grad = jnp.take(pad_zero(gradient), token_of, axis=0).reshape(
        layers_here, tok_count, per_dev, CAP, width
    )
    received_grad = lax.all_to_all(send_grad, "tok", split_axis=1, concat_axis=1, tiled=True)
    projected_slots = jnp.einsum(
        "lspcd,lpjd->lspcj", received_grad, panel_weights, preferred_element_type=jnp.float32
    ).astype(jnp.bfloat16)
    coming_back = lax.all_to_all(
        projected_slots, "tok", split_axis=1, concat_axis=1, tiled=True
    ).reshape(layers_here, PANELS * CAP, panel)
    picked = jax.vmap(take_rows)(coming_back, slot_ids).reshape(layers_here, count, kact, panel)
    attribution_rows = masked.astype(jnp.float32) * picked.astype(jnp.float32)
    scores = attribution_rows.astype(jnp.bfloat16)
    members = (request_ids[:, None] == jnp.arange(REQUESTS, dtype=jnp.int32)[None, :]).astype(
        jnp.float32
    )
    panel_hot = (block_ids[..., None] == jnp.arange(PANELS, dtype=jnp.int32)).astype(jnp.float32)
    local_totals = jnp.einsum(
        "tr,ltkn,ltkj->rlnj", members, panel_hot, attribution_rows, precision=lax.Precision.HIGHEST
    )
    local_totals = local_totals.reshape(REQUESTS, layers_here, PANELS * panel)
    request_totals = lax.psum_scatter(local_totals, "tok", scatter_dimension=2, tiled=True)
    return (scores, request_totals)


def solution(mesh):
    placed = (
        P("lyr", "tok", None, None),
        P("lyr", "tok", None),
        P("tok"),
        P("tok"),
        P("tok", None),
        P("lyr", "tok", None),
    )
    return jax.shard_map(
        per_device,
        mesh=mesh,
        in_specs=placed,
        out_specs=(P("lyr", "tok", None, None), P(None, "lyr", "tok")),
        check_vma=False,
    )
```

profile of v0, /device:TPU:8, one launch (start us, length us, event | category | flops | bytes accessed | tf_op | source)
XLA Modules:
  0.0 573.8 jit_solution(13679655794225082904)
XLA Ops:
  11.0 24.5 %scatter_fusion = s32[2,512]{1,0:T(2,128)S(1)} fusion(s32[2,512]{1,0:T(2,128)S(1)} %broadcast_in_dim.67, s32[512]{0:T(512)S(1)} %bitcast.100, s32[512]{0:T(512)S(1)} %bitcast.109), kind=kCustom, calls=%fused_computation.4 | custom fusion | bytes 10240 | tf_op jit(solution)/shard_map/vmap()/scatter | solution.py:20
  36.8 10.3 %gather_fusion.1 = bf16[1024,256]{1,0:T(8,128)(2,1)} fusion(bf16[2,257,256]{2,0,1:T(2,128)(2,1)S(1)} %concatenate.6, s32[1024]{0:T(1024)S(1)} %bitcast.99), kind=kCustom, calls=%fused_computation.1 | custom fusion | bytes 1056768 | tf_op jit(solution)/shard_map/vmap(jit(_take))/gather | solution.py:24
  48.4 28.2 %all_to_all.20 = bf16[2,32,1,16,256]{4,3,0,2,1:T(8,128)(2,1)S(1)} all-to-all(bf16[2,32,1,16,256]{4,3,0,2,1:T(8,128)(2,1)S(1)} %copy_select_fusion.1), channel_id=1, replica_groups=mesh['tok'=32,'lyr'=8] {'tok'}, dimensions={1} | all-to-all | bytes 1048576 | tf_op jit(solution)/shard_map/all_to_all | solution.py:56
  78.0 2.7 copy.88
  80.7 5.5 all-to-all-start.1
  86.5 107.6 %all-to-all-done.1 = bf16[2,32,1,16,2304]{4,3,0,2,1:T(8,128)(2,1)} async-done(((bf16[2,32,1,16,2304]{4,3,0,2,1:T(8,128)(2,1)}), bf16[2,32,1,16,2304]{4,3,0,2,1:T(8,128)(2,1)}, u32[]{:S(2)}, u32[]{:S(2)}) %all-to-all-start.1) | async-done | bytes 4718624 | tf_op jit(solution)/shard_map/all_to_all | solution.py:60
  194.1 4.9 copy.89
  199.0 13.5 %gather_fusion.2 = bf16[512,2304]{1,0:T(8,128)(2,1)} fusion(bf16[2,512,2304]{2,1,0:T(8,128)(2,1)} %bitcast.98, s32[512]{0:T(512)S(1)} %bitcast.96), kind=kCustom, calls=%fused_computation.2 | custom fusion | bytes 4722688 | tf_op jit(solution)/shard_map/vmap(jit(_take))/gather | solution.py:24
  212.4 3.7 convert_reduce_fusion
  216.2 3.8 reduce_sum.42
  219.9 5.5 reduce_sum.43
  225.6 78.2 %all-reduce.4.cloned.1.call-done = f32[128,2304]{1,0:T(8,128)} async-done(((f32[128,2304]{1,0:T(8,128)}), f32[128,2304]{1,0:T(8,128)}) %all-reduce.4.cloned.1.call-update) | async-done | bytes 1179664 | tf_op jit(solution)/shard_map/psum | solution.py:67
  303.8 1.6 multiply_reduce_fusion
  305.7 6.2 %gather_fusion = bf16[1024,2304]{1,0:T(8,128)(2,1)} fusion(bf16[129,2304]{1,0:T(8,128)(2,1)S(1)} %concatenate.7, s32[1024]{0:T(1024)S(1)} %broadcast_clamp_fusion), kind=kCustom, calls=%fused_computation | custom fusion | bytes 9441280 | tf_op jit(solution)/shard_map/jit(_take)/gather | solution.py:69
  311.9 2.8 copy_select_fusion
  314.8 99.7 %all_to_all.21 = bf16[2,32,1,16,2304]{4,3,0,2,1:T(8,128)(2,1)S(1)} all-to-all(bf16[2,32,1,16,2304]{4,3,0,2,1:T(8,128)(2,1)S(1)} %copy_select_fusion), channel_id=1, replica_groups=mesh['tok'=32,'lyr'=8] {'tok'}, dimensions={1} | all-to-all | bytes 9437184 | tf_op jit(solution)/shard_map/all_to_all | solution.py:72
  414.4 1.4 fusion.16
  416.7 21.7 %all-to-all-start.3 = ((bf16[2,32,1,16,256]{4,3,0,2,1:T(8,128)(2,1)}), bf16[2,32,1,16,256]{4,3,0,2,1:T(8,128)(2,1)}, u32[]{:S(2)}, u32[]{:S(2)}) async-start(bf16[2,32,1,16,256]{4,3,0,2,1:T(8,128)(2,1)} %copy.93), calls=%async_computation.3 | async-start | bytes 1048576 | tf_op jit(solution)/shard_map/all_to_all | solution.py:76
  439.1 17.3 %all-to-all-done.3 = bf16[2,32,1,16,256]{4,3,0,2,1:T(8,128)(2,1)} async-done(((bf16[2,32,1,16,256]{4,3,0,2,1:T(8,128)(2,1)}), bf16[2,32,1,16,256]{4,3,0,2,1:T(8,128)(2,1)}, u32[]{:S(2)}, u32[]{:S(2)}) %all-to-all-start.3) | async-done | bytes 524320 | tf_op jit(solution)/shard_map/all_to_all | solution.py:76
  457.5 5.6 gather_fusion.3
  464.2 5.6 fusion.23
  469.7 7.5 %fusion.8 = f32[2,32,2,8,256]{4,3,2,1,0:T(8,128)S(1)} fusion(f32[2,128,256,32]{2,3,1,0:T(8,128)S(1)} %fusion.23, s32[128]{0:T(128)S(1)} %copy-done.6), kind=kOutput, calls=%fused_computation.16 | convolution fusion | flops 402655232 | bytes 9437696 | tf_op jit(solution)/shard_map/tr,ltkn,ltkj->rlnj/dot_general | solution.py:86
  479.8 85.7 %reduce-scatter.2.cloned.1.call-done = f32[16,2,256]{2,0,1:T(8,128)} async-done(((f32[16,2,8192]{2,0,1:T(8,128)}), f32[16,2,256]{2,0,1:T(8,128)}) %reduce-scatter.2.cloned.1.call-update) | async-done | bytes 32784 | tf_op jit(solution)/shard_map/reduce_scatter | solution.py:90
  565.5 1.4 copy.98
  (67 shorter events, 14.4 us)
Async XLA Ops:
  7.2 69.4 %copy-start = (bf16[2,256,2304]{2,1,0:T(8,128)(2,1)S(1)}, bf16[2,256,2304]{2,1,0:T(8,128)(2,1)}, u32[]{:S(2)}) copy-start(bf16[2,256,2304]{2,1,0:T(8,128)(2,1)} %param.11) | copy-start | bytes 7077892
  10.7 24.9 %copy-start.7 = (s32[128]{0:T(128)S(1)}, s32[128]{0:T(128)}, u32[]{:S(2)}) copy-start(s32[128]{0:T(128)} %param.8) | copy-start | bytes 1540
  10.7 25.0 %copy-start.3 = (bf16[2,128,2,256]{3,2,1,0:T(2,128)(2,1)S(1)}, bf16[2,128,2,256]{3,2,1,0:T(2,128)(2,1)}, u32[]{:S(2)}) copy-start(bf16[2,128,2,256]{3,2,1,0:T(2,128)(2,1)} %param.6) | copy-start | bytes 786436
  80.7 113.4 %all-to-all-start.1 = ((bf16[2,32,1,16,2304]{4,3,0,2,1:T(8,128)(2,1)}), bf16[2,32,1,16,2304]{4,3,0,2,1:T(8,128)(2,1)}, u32[]{:S(2)}, u32[]{:S(2)}) async-start(bf16[2,32,1,16,2304]{4,3,0,2,1:T(8,128)(2,1)} %copy.88), calls=%async_computation.1 | async-start | bytes 9437184 | tf_op jit(solution)/shard_map/all_to_all | solution.py:60
  86.2 217.6 %all-reduce.4.cloned.1.call-start = ((), (), s32[]{:S(2)}) async-start(), calls=%async_computation.5 | async-start | bytes 2359296 | tf_op jit(solution)/shard_map/psum | solution.py:67
  219.9 83.9 %copy-start.2 = (bf16[128,2304]{1,0:T(8,128)(2,1)S(1)}, bf16[128,2304]{1,0:T(8,128)(2,1)}, u32[]{:S(2)}) copy-start(bf16[128,2304]{1,0:T(8,128)(2,1)} %param.10) | copy-start | bytes 1769476
  303.8 1.6 copy-start.1
  415.8 23.0 %copy-start.5 = (s32[2,128,2]{1,2,0:T(2,128)S(1)}, s32[2,128,2]{1,2,0:T(2,128)}, u32[]{:S(2)}) copy-start(s32[2,128,2]{1,2,0:T(2,128)} %param.7) | copy-start | bytes 6148
  416.7 39.7 %all-to-all-start.3 = ((bf16[2,32,1,16,256]{4,3,0,2,1:T(8,128)(2,1)}), bf16[2,32,1,16,256]{4,3,0,2,1:T(8,128)(2,1)}, u32[]{:S(2)}, u32[]{:S(2)}) async-start(bf16[2,32,1,16,256]{4,3,0,2,1:T(8,128)(2,1)} %copy.93), calls=%async_computation.3 | async-start | bytes 1048576 | tf_op jit(solution)/shard_map/all_to_all | solution.py:76
  438.4 127.1 %reduce-scatter.2.cloned.1.call-start = ((), (), s32[]{:S(2)}) async-start(), calls=%async_computation.6 | async-start | bytes 1081344 | tf_op jit(solution)/shard_map/reduce_scatter | solution.py:90
  464.1 5.6 copy-start.6
  477.3 1.1 copy-start.4
Sparse Core Ops, SparseCore 0:
  225.6 78.1 all-reduce.3
  478.5 86.9 reduce-scatter.1
where the time goes:
time: 575 us; the launch traced here: 574 us
  waiting for transfers between devices  289 us (50%)
  blocking collectives  128 us (22%)
  local copies, waits for them, and re-layouts  80 us (14%)
  starting transfers between devices  27.6 us (5%)
  other arithmetic  19.1 us (3%)
  matrix products  15.9 us (3%)
  between operations  14.4 us (3%)
    all_to_all x1, waiting for transfers between devices, per_device(): lax.all_to_all(built, 'tok', split_axis=1, concat_axis=1, tiled=True)  108 us
    all_to_all x1, blocking collectives, per_device(): lax.all_to_all(send_grad, 'tok', split_axis=1, concat_axis=1, tiled=True)  99.7 us
    reduce_scatter x1, waiting for transfers between devices, per_device(): lax.psum_scatter(local_totals, 'tok', scatter_dimension=2, tiled=True)  85.7 us
    psum x1, waiting for transfers between devices, per_device(): rebuilt = lax.psum(partial_value, 'lyr')  78.2 us
    gather x4, local copies, waits for them, and re-layouts, take_rows(): return jnp.take(table, index, axis=0)  30.4 us
    all_to_all x1, blocking collectives, per_device(): lax.all_to_all(send_codes, 'tok', split_axis=1, concat_axis=1, tiled=True)  28.2 us
    scatter x1, local copies, waits for them, and re-layouts, source_of(): return empty.at[slot_ids].set(jnp.arange(row_count, dtype=jnp.int32))  24.5 us
    all_to_all x1, starting transfers between devices, per_device(): lax.all_to_all(projected_slots, 'tok', split_axis=1, concat_axis=1, tiled...  21.7 us
  transfers between devices with their start and end apart: 4, of which 4 were waited for; matrix products, arithmetic and copies ran while one was open for 0% of the time, Pallas kernels for 0%

commit v1 on v0

--- a/solution.py
+++ b/solution.py
@@ -64,7 +64,7 @@
     partial_value = jnp.sum(
         per_row.astype(jnp.float32).reshape(layers_here, count, kact, width), axis=(0, 2)
     )
-    rebuilt = lax.psum(partial_value, "lyr")
+    rebuilt = jnp.sum(lax.all_gather(partial_value, "lyr"), axis=0)
     gradient = normalize_error(target_resid, rebuilt)
     send_grad = jnp.take(pad_zero(gradient), token_of, axis=0).reshape(
         layers_here, tok_count, per_dev, CAP, width

time: 575 us -> 593 us (1.031)
  waiting for transfers between devices: 289 us -> 307 us
  blocking collectives: 128 us -> 145 us
  starting transfers between devices: 27.6 us -> 12 us
  local copies, waits for them, and re-layouts: 80 us -> 73.7 us
    all_gather x0 -> x1, waiting for transfers between devices: none -> 98.7 us  [per_device(): rebuilt = jnp.sum(lax.all_gather(partial_value, 'lyr'), axis=0)]
    psum x1 -> x0, waiting for transfers between devices: 78.2 us -> none  [per_device(): rebuilt = lax.psum(partial_value, 'lyr')]
    all_to_all x1, blocking collectives: 99.7 us -> 117 us  [per_device(): lax.all_to_all(send_grad, 'tok', split_axis=1, concat_axis=1, tiled=True)]
    all_to_all x1, starting transfers between devices: 21.7 us -> 5.97 us  [per_device(): lax.all_to_all(projected_slots, 'tok', split_axis=1, concat_axis=1, tiled...]
    gather x4, local copies, waits for them, and re-layouts: 30.4 us -> 22.2 us  [take_rows(): return jnp.take(table, index, axis=0)]
  transfers between devices with their start and end apart: 4 -> 4, of which waited for: 4 -> 4; matrix products, arithmetic and copies ran while one was open for 0% -> 1% of each run, Pallas kernels for 0% -> 0%
where the time goes in v1:
time: 593 us; the launch traced here: 592 us
  waiting for transfers between devices  307 us (52%)
  blocking collectives  145 us (24%)
  local copies, waits for them, and re-layouts  73.7 us (12%)
  other arithmetic  23.1 us (4%)
  matrix products  16.7 us (3%)
  between operations  14.5 us (2%)
  starting transfers between devices  12 us (2%)
    all_to_all x1, blocking collectives, per_device(): lax.all_to_all(send_grad, 'tok', split_axis=1, concat_axis=1, tiled=True)  117 us
    all_to_all x1, waiting for transfers between devices, per_device(): lax.all_to_all(built, 'tok', split_axis=1, concat_axis=1, tiled=True)  108 us
    all_gather x1, waiting for transfers between devices, per_device(): rebuilt = jnp.sum(lax.all_gather(partial_value, 'lyr'), axis=0)  98.7 us
    reduce_scatter x1, waiting for transfers between devices, per_device(): lax.psum_scatter(local_totals, 'tok', scatter_dimension=2, tiled=True)  84.6 us
    all_to_all x1, blocking collectives, per_device(): lax.all_to_all(send_codes, 'tok', split_axis=1, concat_axis=1, tiled=True)  28.2 us
    scatter x1, local copies, waits for them, and re-layouts, source_of(): return empty.at[slot_ids].set(jnp.arange(row_count, dtype=jnp.int32))  24.5 us
    gather x4, local copies, waits for them, and re-layouts, take_rows(): return jnp.take(table, index, axis=0)  22.2 us
    all_to_all x1, waiting for transfers between devices, per_device(): lax.all_to_all(projected_slots, 'tok', split_axis=1, concat_axis=1, tiled...  15.8 us
  transfers between devices with their start and end apart: 4, of which 4 were waited for; matrix products, arithmetic and copies ran while one was open for 1% of the time, Pallas kernels for 0%

profile of v1, /device:TPU:8, one launch (start us, length us, event | category | flops | bytes accessed | tf_op | source)
XLA Modules:
  0.0 591.7 jit_solution(11829020585713474713)
XLA Ops:
  11.1 24.5 %scatter_fusion = s32[2,512]{1,0:T(2,128)S(1)} fusion(s32[2,512]{1,0:T(2,128)S(1)} %broadcast_in_dim.67, s32[512]{0:T(512)S(1)} %bitcast.101, s32[512]{0:T(512)S(1)} %bitcast.111), kind=kCustom, calls=%fused_computation.4 | custom fusion | bytes 10240 | tf_op jit(solution)/shard_map/vmap()/scatter | solution.py:20
  37.5 5.5 gather_fusion.1
  43.2 28.2 %all_to_all.20 = bf16[2,32,1,16,256]{4,3,0,2,1:T(8,128)(2,1)S(1)} all-to-all(bf16[2,32,1,16,256]{4,3,0,2,1:T(8,128)(2,1)S(1)} %copy_select_fusion.1), channel_id=1, replica_groups=mesh['tok'=32,'lyr'=8] {'tok'}, dimensions={1} | all-to-all | bytes 1048576 | tf_op jit(solution)/shard_map/all_to_all | solution.py:56
  72.9 2.7 copy.88
  75.6 5.5 all-to-all-start.1
  81.4 107.6 %all-to-all-done.1 = bf16[2,32,1,16,2304]{4,3,0,2,1:T(8,128)(2,1)} async-done(((bf16[2,32,1,16,2304]{4,3,0,2,1:T(8,128)(2,1)}), bf16[2,32,1,16,2304]{4,3,0,2,1:T(8,128)(2,1)}, u32[]{:S(2)}, u32[]{:S(2)}) %all-to-all-start.1) | async-done | bytes 4718624 | tf_op jit(solution)/shard_map/all_to_all | solution.py:60
  189.0 4.9 copy.89
  193.8 13.5 %gather_fusion.2 = bf16[512,2304]{1,0:T(8,128)(2,1)} fusion(bf16[2,512,2304]{2,1,0:T(8,128)(2,1)} %bitcast.99, s32[512]{0:T(512)S(1)} %bitcast.97), kind=kCustom, calls=%fused_computation.2 | custom fusion | bytes 4722688 | tf_op jit(solution)/shard_map/vmap(jit(_take))/gather | solution.py:24
  207.3 3.7 convert_reduce_fusion
  211.1 3.8 reduce_sum.51
  214.8 5.5 reduce_sum.52
  221.0 98.7 %all-gather.3.cloned.1.call-done = f32[1024,2304]{1,0:T(8,128)} async-done(((f32[128,2304]{1,0:T(8,128)}), f32[1024,2304]{1,0:T(8,128)}) %all-gather.3.cloned.1.call-update) | async-done | bytes 9437200 | tf_op jit(solution)/shard_map/all_gather | solution.py:67
  319.7 4.4 reduce_sum.53
  326.8 6.2 %gather_fusion = bf16[1024,2304]{1,0:T(8,128)(2,1)} fusion(bf16[129,2304]{1,0:T(8,128)(2,1)S(1)} %concatenate.7, s32[1024]{0:T(1024)S(1)} %broadcast_clamp_fusion), kind=kCustom, calls=%fused_computation | custom fusion | bytes 9441280 | tf_op jit(solution)/shard_map/jit(_take)/gather | solution.py:69
  333.0 2.8 copy_select_fusion
  335.8 116.9 %all_to_all.21 = bf16[2,32,1,16,2304]{4,3,0,2,1:T(8,128)(2,1)S(1)} all-to-all(bf16[2,32,1,16,2304]{4,3,0,2,1:T(8,128)(2,1)S(1)} %copy_select_fusion), channel_id=1, replica_groups=mesh['tok'=32,'lyr'=8] {'tok'}, dimensions={1} | all-to-all | bytes 9437184 | tf_op jit(solution)/shard_map/all_to_all | solution.py:72
  452.7 1.4 fusion.16
  455.0 6.0 %all-to-all-start.3 = ((bf16[2,32,1,16,256]{4,3,0,2,1:T(8,128)(2,1)}), bf16[2,32,1,16,256]{4,3,0,2,1:T(8,128)(2,1)}, u32[]{:S(2)}, u32[]{:S(2)}) async-start(bf16[2,32,1,16,256]{4,3,0,2,1:T(8,128)(2,1)} %copy.93), calls=%async_computation.3 | async-start | bytes 1048576 | tf_op jit(solution)/shard_map/all_to_all | solution.py:76
  462.3 15.8 %all-to-all-done.3 = bf16[2,32,1,16,256]{4,3,0,2,1:T(8,128)(2,1)} async-done(((bf16[2,32,1,16,256]{4,3,0,2,1:T(8,128)(2,1)}), bf16[2,32,1,16,256]{4,3,0,2,1:T(8,128)(2,1)}, u32[]{:S(2)}, u32[]{:S(2)}) %all-to-all-start.3) | async-done | bytes 524320 | tf_op jit(solution)/shard_map/all_to_all | solution.py:76
  479.2 3.2 gather_fusion.3
  482.5 6.3 %fusion.23 = f32[2,128,256,32]{2,3,1,0:T(8,128)S(1)} fusion(bf16[2,128,2,256]{3,2,1,0:T(2,128)(2,1)S(1)} %copy-done.2, s32[2,128,2]{2,1,0:T(8,128)S(1)} %copy-done.4, bf16[2,128,2,256]{3,2,1,0:T(2,128)(2,1)S(1)} %gather.28, pred[2,128,2]{2,1,0:T(8,128)(4,1)} %copy.81), kind=kOutput, calls=%fused_computation.26 | convolution fusion | flops 50872320 | bytes 8915456 | tf_op jit(solution)/shard_map/tr,ltkn,ltkj->rlnj/dot_general | solution.py:86
  488.9 7.5 %fusion.8 = f32[2,32,2,8,256]{4,3,2,1,0:T(8,128)S(1)} fusion(f32[2,128,256,32]{2,3,1,0:T(8,128)S(1)} %fusion.23, s32[128]{0:T(128)S(1)} %copy-done.10), kind=kOutput, calls=%fused_computation.16 | convolution fusion | flops 402655232 | bytes 9437696 | tf_op jit(solution)/shard_map/tr,ltkn,ltkj->rlnj/dot_general | solution.py:86
  498.9 84.6 %reduce-scatter.2.cloned.1.call-done = f32[16,2,256]{2,0,1:T(8,128)} async-done(((f32[16,2,8192]{2,0,1:T(8,128)}), f32[16,2,256]{2,0,1:T(8,128)}) %reduce-scatter.2.cloned.1.call-update) | async-done | bytes 32784 | tf_op jit(solution)/shard_map/reduce_scatter | solution.py:90
  583.5 1.4 copy.98
  (76 shorter events, 16.7 us)
Async XLA Ops:
  7.2 64.3 %copy-start = (bf16[2,256,2304]{2,1,0:T(8,128)(2,1)S(1)}, bf16[2,256,2304]{2,1,0:T(8,128)(2,1)}, u32[]{:S(2)}) copy-start(bf16[2,256,2304]{2,1,0:T(8,128)(2,1)} %param.11) | copy-start | bytes 7077892
  8.1 2.9 copy-start.3
  10.7 24.9 %copy-start.11 = (s32[128]{0:T(128)S(1)}, s32[128]{0:T(128)}, u32[]{:S(2)}) copy-start(s32[128]{0:T(128)} %param.8) | copy-start | bytes 1540
  10.7 25.0 %copy-start.5 = (bf16[2,128,2,256]{3,2,1,0:T(2,128)(2,1)S(1)}, bf16[2,128,2,256]{3,2,1,0:T(2,128)(2,1)}, u32[]{:S(2)}) copy-start(bf16[2,128,2,256]{3,2,1,0:T(2,128)(2,1)} %param.6) | copy-start | bytes 786436
  36.1 0.7 copy-start.1
  75.6 113.4 %all-to-all-start.1 = ((bf16[2,32,1,16,2304]{4,3,0,2,1:T(8,128)(2,1)}), bf16[2,32,1,16,2304]{4,3,0,2,1:T(8,128)(2,1)}, u32[]{:S(2)}, u32[]{:S(2)}) async-start(bf16[2,32,1,16,2304]{4,3,0,2,1:T(8,128)(2,1)} %copy.88), calls=%async_computation.1 | async-start | bytes 9437184 | tf_op jit(solution)/shard_map/all_to_all | solution.py:60
  81.1 238.6 %all-gather.3.cloned.1.call-start = ((), (), s32[]{:S(2)}) async-start(), calls=%async_computation.6 | async-start | bytes 10616832 | tf_op jit(solution)/shard_map/all_gather | solution.py:67
  326.8 6.2 %copy-start.8 = (pred[2,32,16]{2,0,1:T(4,128)(4,1)S(1)}, pred[2,32,16]{2,0,1:T(4,128)(4,1)}, u32[]{:S(2)}) copy-start(pred[2,32,16]{2,0,1:T(4,128)(4,1)} %copy.83) | copy-start | bytes 3076
  454.1 7.4 %copy-start.9 = (s32[2,128,2]{1,2,0:T(2,128)S(1)}, s32[2,128,2]{1,2,0:T(2,128)}, u32[]{:S(2)}) copy-start(s32[2,128,2]{1,2,0:T(2,128)} %param.7) | copy-start | bytes 6148
  455.0 23.1 %all-to-all-start.3 = ((bf16[2,32,1,16,256]{4,3,0,2,1:T(8,128)(2,1)}), bf16[2,32,1,16,256]{4,3,0,2,1:T(8,128)(2,1)}, u32[]{:S(2)}, u32[]{:S(2)}) async-start(bf16[2,32,1,16,256]{4,3,0,2,1:T(8,128)(2,1)} %copy.93), calls=%async_computation.3 | async-start | bytes 1048576 | tf_op jit(solution)/shard_map/all_to_all | solution.py:76
  461.0 21.5 %copy-start.2 = (bf16[2,128,2,256]{3,2,1,0:T(2,128)(2,1)S(1)}, bf16[2,128,2,256]{3,2,1,0:T(2,128)(2,1)}, u32[]{:S(2)}) copy-start(bf16[2,128,2,256]{3,2,1,0:T(2,128)(2,1)} %copy-done.1) | copy-start | bytes 786436
  461.0 21.5 %copy-start.4 = (s32[2,128,2]{2,1,0:T(8,128)S(1)}, s32[2,128,2]{2,1,0:T(8,128)}, u32[]{:S(2)}) copy-start(s32[2,128,2]{2,1,0:T(8,128)} %copy-done.3) | copy-start | bytes 6148
  461.0 122.5 %reduce-scatter.2.cloned.1.call-start = ((), (), s32[]{:S(2)}) async-start(), calls=%async_computation.5 | async-start | bytes 1081344 | tf_op jit(solution)/shard_map/reduce_scatter | solution.py:90
  482.5 6.3 %copy-start.10 = (s32[128]{0:T(128)S(1)}, s32[128]{0:T(128)}, u32[]{:S(2)}) copy-start(s32[128]{0:T(128)} %param.9) | copy-start | bytes 1540
  496.4 1.1 copy-start.6
  496.4 1.1 copy-start.7
Sparse Core Ops, SparseCore 0:
  220.4 99.2 all-gather.2
  497.6 85.8 reduce-scatter.1
